TPU v7x, 32 devices: a whole 2x2x4 slice. The times are simulated.
32 devices in a mesh: groups: 2 (over x), blk: 4 (over y, core), width: 4 (over z).
Axes of the slice: x: 2, y: 2, z: 4, core: 2. Of those that a mesh axis runs over, the one named last changes fastest.
Arguments:
- activations: float32 [8192, 8192], P(('groups', 'blk'), 'width'), parts along dimension 0, may hold values from -6 to 6
- query_grads: float32 [16, 8192, 128], P(('groups', 'blk'), 'width'), parts along dimension 0, may hold values from -0.0625 to 0.0625
- outgrad_proj: float32 [8192, 128], P(('groups', 'blk', 'width')), parts along dimension 0, may hold values from -0.6 to 0.6
- doc_ids: int32 [8192], P(('groups', 'blk', 'width')), parts along dimension 0, may hold values from 0 to 15, never falling along the last dimension, each value on 1 to 512 neighbouring positions
Outputs:
- token_scores: float32 [8192, 8], P(('groups', 'blk', 'width')), parts along dimension 0
- doc_scores: float32 [32, 8], P('groups'), parts along dimension 0
There are 2 independent parts, one for each index of `groups`. A program takes and returns all parts, laid end to end along the dimension named above; each array names one. Nothing has to cross between parts.
Inputs may be any that keep to these rules, and one draw needn't show every extreme that they name: `doc_ids`: never falls along the tokens; every document 0 to 15 holds 1 to 512 tokens, one exactly 512.
All inputs are finite; a program needn't handle non-finite values.
Results may differ from a plain program's by a relative error of at most 0.000078.
Values sent between devices are 32-bit elements; how exact they have to be, the bound alone decides.
No kernel may reach another device: no remote copies, remote signals or barrier semaphores. Data moves between devices by JAX's collectives and lax.ppermute only.
A program may use at most 128 MiB of HBM per device.

v0:
```python
import jax
import jax.numpy as jnp
from jax import lax
from jax.sharding import PartitionSpec as P

DOC_BLK = 4


def per_device(activations, query_grads, outgrad_proj, doc_ids):
    projected = jnp.einsum(
        "td,qdr->tqr",
        activations,
        lax.all_gather(query_grads, "blk", axis=0, tiled=True),
        precision=lax.Precision.HIGHEST,
        preferred_element_type=jnp.float32,
    )
    owned_parts = lax.psum_scatter(projected, "width", scatter_dimension=0, tiled=True)
    token_scores = jnp.sum(owned_parts * outgrad_proj[:, None, :], axis=2)
    doc_total = DOC_BLK * lax.axis_size("blk")
    doc_range = jnp.arange(doc_total, dtype=jnp.int32)
    onehot = (doc_ids[:, None] == doc_range[None, :]).astype(jnp.float32)
    doc_sums = jnp.einsum(
        "tn,tq->nq",
        onehot,
        token_scores,
        precision=lax.Precision.HIGHEST,
        preferred_element_type=jnp.float32,
    )
    doc_counts = jnp.sum(onehot, axis=0)
    doc_sums, doc_counts = lax.psum((doc_sums, doc_counts), ("blk", "width"))
    doc_scores = doc_sums / jnp.sqrt(doc_counts)[:, None]
    return (token_scores, doc_scores)


def solution(mesh):
    return jax.shard_map(
        per_device,
        mesh=mesh,
        in_specs=(
            P(("groups", "blk"), "width"),
            P(("groups", "blk"), "width", None),
            P(("groups", "blk", "width"), None),
            P(("groups", "blk", "width")),
        ),
        out_specs=(P(("groups", "blk", "width"), None), P("groups", None)),
        check_vma=False,
    )
```

profile of v0, /device:TPU:0, one launch (start us, length us, event | category | flops | bytes accessed | tf_op | source)
XLA Modules:
  0.0 222.9 jit_solution(11770008080408502427)
XLA Ops:
  7.2 0.0 all-gather.2.cloned.1.call-start
  7.2 0.7 all-gather.2.cloned.1.call-update
  7.9 0.0 copy-start.2
  7.9 0.0 copy-start
  7.9 0.0 reduce-scatter.2.cloned.1.call-start
  8.0 62.6 %all-gather.2.cloned.1.call-done = f32[8,2048,128]{2,1,0:T(8,128)} async-done(((f32[2,2048,128]{2,1,0:T(8,128)}), f32[8,2048,128]{2,1,0:T(8,128)}) %all-gather.2.cloned.1.call-update) | async-done | bytes 8388624 | tf_op jit(solution)/shard_map/all_gather | solution.py:13
  70.6 32.7 %fusion = f32[1024,8,128]{2,0,1:T(8,128)} fusion(f32[8,2048,128]{2,1,0:T(8,128)} %all-gather.2.cloned.1.call-done, f32[1024,2048]{1,0:T(8,128)} %param.4), kind=kOutput, calls=%fused_computation | convolution fusion | flops 25769803776 | bytes 20971520 | tf_op jit(solution)/shard_map/td,qdr->tqr/dot_general | solution.py:10
  103.3 0.0 reduce-scatter.2.cloned.1.call-update
  103.3 0.0 copy-done.2
  103.3 0.1 convert_reduce_fusion
  103.4 76.8 %reduce-scatter.2.cloned.1.call-done = f32[256,8,128]{2,0,1:T(8,128)} async-done(((f32[1024,8,128]{2,0,1:T(8,128)}), f32[256,8,128]{2,0,1:T(8,128)}) %reduce-scatter.2.cloned.1.call-update) | async-done | bytes 1048592 | tf_op jit(solution)/shard_map/reduce_scatter | solution.py:17
  180.2 0.0 copy-done
  180.2 1.6 multiply_reduce_fusion
  181.8 0.0 copy-start.1
  181.8 0.1 fusion.2
  181.9 33.5 %all-reduce = (f32[16,8]{0,1:T(8,128)S(1)}, f32[16]{0:T(128)S(1)}) all-reduce(f32[16,8]{0,1:T(8,128)S(1)} %fusion.2, f32[16]{0:T(128)S(1)} %convert_reduce_fusion), channel_id=1, replica_groups=mesh['groups'=2,'blk'=4,'width'=4] {'blk','width'}, use_global_device_ids=true, to_apply=%region_2.0 | all-reduce | flops 144 | bytes 1152 | tf_op jit(solution)/shard_map/psum | solution.py:30
  215.5 0.6 broadcast_divide_fusion
  216.1 0.0 copy-done.1
  (1 shorter events, 0.0 us)
Async XLA Ops:
  7.2 63.4 %all-gather.2.cloned.1.call-start = ((), (), s32[]{:S(2)}) async-start(), calls=%async_computation.1 | async-start | bytes 10485760 | tf_op jit(solution)/shard_map/all_gather | solution.py:13
  7.9 95.4 %copy-start.2 = (s32[256]{0:T(256)S(1)}, s32[256]{0:T(256)}, u32[]{:S(2)}) copy-start(s32[256]{0:T(256)} %param.7) | copy-start | bytes 3076
  7.9 172.3 %copy-start = (f32[256,128]{1,0:T(8,128)S(1)}, f32[256,128]{1,0:T(8,128)}, u32[]{:S(2)}) copy-start(f32[256,128]{1,0:T(8,128)} %param.6) | copy-start | bytes 393220
  7.9 172.3 %reduce-scatter.2.cloned.1.call-start = ((), (), s32[]{:S(2)}) async-start(), calls=%async_computation.2 | async-start | bytes 5242880 | tf_op jit(solution)/shard_map/reduce_scatter | solution.py:17
  181.8 34.3 %copy-start.1 = (f32[256,8]{0,1:T(8,128)}, f32[256,8]{0,1:T(8,128)S(1)}, u32[]{:S(2)}) copy-start(f32[256,8]{0,1:T(8,128)S(1)} %multiply_reduce_fusion) | copy-start | bytes 24580
Sparse Core Ops, SparseCore 0:
  9.6 60.9 all-gather.1
  103.4 76.7 reduce-scatter.1
where the time goes:
time: 223 us
  waiting for transfers between devices  140 us (63%)
  blocking collectives  33.5 us (15%)
  matrix products  32.8 us (15%)
  between operations  14.1 us (6%)
  other arithmetic  2.29 us (1%)
    reduce_scatter x1, waiting for transfers between devices, per_device(): lax.psum_scatter(projected, 'width', scatter_dimension=0, tiled=True)  76.8 us
    all_gather x1, waiting for transfers between devices, per_device(): lax.all_gather(query_grads, 'blk', axis=0, tiled=True)  62.6 us
    psum x1, blocking collectives, per_device(): doc_sums, doc_counts = lax.psum((doc_sums, doc_counts), ('blk', 'width'))  33.5 us
    dot_general x1, matrix products, per_device(): jnp.einsum('td,qdr->tqr', activations, lax.all_gather(query_grads, 'blk',...  32.7 us
  transfers between devices with their start and end apart: 2, of which 2 were waited for; matrix products, arithmetic and copies ran while one was open for 0% of the time, Pallas kernels for 0%

commit v1 on v0

--- a/solution.py
+++ b/solution.py
@@ -7,13 +7,27 @@
 
 
 def per_device(activations, query_grads, outgrad_proj, doc_ids):
-    projected = jnp.einsum(
-        "td,qdr->tqr",
-        activations,
-        lax.all_gather(query_grads, "blk", axis=0, tiled=True),
-        precision=lax.Precision.HIGHEST,
-        preferred_element_type=jnp.float32,
-    )
+    x = query_grads
+    ways, here, lap = (lax.axis_size("blk"), lax.axis_index("blk"), x.shape[0])
+    results = []
+    for far in range(ways):
+        arriving = (
+            lax.ppermute(x, "blk", [(d, (d + 1) % ways) for d in range(ways)])
+            if far + 1 < ways
+            else x
+        )
+        results.append(
+            jnp.einsum(
+                "td,qdr->tqr",
+                activations,
+                x,
+                precision=lax.Precision.HIGHEST,
+                preferred_element_type=jnp.float32,
+            )
+        )
+        x = arriving
+    line = jnp.concatenate(results[::-1], axis=1)
+    projected = jnp.roll(line, (here + 1) * results[0].shape[1], axis=1)
     owned_parts = lax.psum_scatter(projected, "width", scatter_dimension=0, tiled=True)
     token_scores = jnp.sum(owned_parts * outgrad_proj[:, None, :], axis=2)
     doc_total = DOC_BLK * lax.axis_size("blk")

time: 223 us -> 241 us (1.081)
  waiting for transfers between devices: 140 us -> 156 us
  local copies, waits for them, and re-layouts: 0.02 us -> 2.53 us
    ppermute x0 -> x3, waiting for transfers between devices: none -> 77.2 us  [per_device(): lax.ppermute(x, 'blk', [(d, (d + 1) % ways) for d in range(ways)])]
    all_gather x1 -> x0, waiting for transfers between devices: 62.6 us -> none  [per_device(): lax.all_gather(query_grads, 'blk', axis=0, tiled=True)]
    dot_general x1 -> x4, matrix products: 32.7 us -> 31.4 us  [per_device(): jnp.einsum('td,qdr->tqr', activations, x, precision=lax.Precision.HIGHEST...]
  transfers between devices with their start and end apart: 2 -> 4, of which waited for: 2 -> 4; matrix products, arithmetic and copies ran while one was open for 0% -> 0% of each run, Pallas kernels for 0% -> 0%
where the time goes in v1:
time: 241 us
  waiting for transfers between devices  156 us (65%)
  blocking collectives  33.5 us (14%)
  matrix products  31.5 us (13%)
  between operations  14.2 us (6%)
  local copies, waits for them, and re-layouts  2.53 us (1%)
    reduce_scatter x1, waiting for transfers between devices, per_device(): lax.psum_scatter(projected, 'width', scatter_dimension=0, tiled=True)  78.8 us
    ppermute x3, waiting for transfers between devices, per_device(): lax.ppermute(x, 'blk', [(d, (d + 1) % ways) for d in range(ways)])  77.2 us
    psum x1, blocking collectives, per_device(): doc_sums, doc_counts = lax.psum((doc_sums, doc_counts), ('blk', 'width'))  33.5 us
    dot_general x4, matrix products, per_device(): jnp.einsum('td,qdr->tqr', activations, x, precision=lax.Precision.HIGHEST...  31.4 us
  transfers between devices with their start and end apart: 4, of which 4 were waited for; matrix products, arithmetic and copies ran while one was open for 0% of the time, Pallas kernels for 0%

profile of v1, /device:TPU:0, one launch (start us, length us, event | category | flops | bytes accessed | tf_op | source)
XLA Modules:
  0.0 240.6 jit_solution(2954230430260356823)
XLA Ops:
  7.2 0.0 reduce-scatter.2.cloned.1.call-start
  7.2 0.5 collective-permute-start
  7.7 25.9 %collective-permute-done = f32[2,2048,128]{2,1,0:T(8,128)S(1)} collective-permute-done((f32[2,2048,128]{2,1,0:T(8,128)}, f32[2,2048,128]{2,1,0:T(8,128)S(1)}, u32[]{:S(2)}, u32[]{:S(2)}) %collective-permute-start) | collective-permute-done | bytes 2097184 | tf_op jit(solution)/shard_map/ppermute | solution.py:15
  33.6 0.0 collective-permute-start.1
  33.6 25.5 %collective-permute-done.1 = f32[2,2048,128]{2,1,0:T(8,128)} collective-permute-done((f32[2,2048,128]{2,1,0:T(8,128)S(1)}, f32[2,2048,128]{2,1,0:T(8,128)}, u32[]{:S(2)}, u32[]{:S(2)}) %collective-permute-start.1) | collective-permute-done | bytes 2097184 | tf_op jit(solution)/shard_map/ppermute | solution.py:15
  59.2 0.0 collective-permute-start.2
  59.2 0.0 copy-start
  59.2 25.8 %collective-permute-done.2 = f32[2,2048,128]{2,1,0:T(8,128)} collective-permute-done((f32[2,2048,128]{2,1,0:T(8,128)}, f32[2,2048,128]{2,1,0:T(8,128)}, u32[]{:S(2)}, u32[]{:S(2)}) %collective-permute-start.2) | collective-permute-done | bytes 2097184 | tf_op jit(solution)/shard_map/ppermute | solution.py:15
  84.9 9.6 %constant_dynamic-update-slice_fusion.7 = (f32[1024,16,128]{2,0,1:T(8,128)S(1)}, f32[1024,2,128]{2,0,1:T(8,128)S(1)}) fusion(f32[2,2048,128]{2,1,0:T(8,128)} %collective-permute-done.2, f32[1024,2048]{1,0:T(8,128)} %param.4), kind=kOutput, calls=%fused_computation.16 | convolution fusion | flops 6442450944 | bytes 12582912 | tf_op jit(solution)/shard_map/td,qdr->tqr/dot_general | solution.py:20
  94.5 0.0 copy-done
  94.6 8.2 %constant_dynamic-update-slice_fusion.6 = (f32[1024,16,128]{2,0,1:T(8,128)S(1)}, f32[1024,2,128]{2,0,1:T(8,128)S(1)}) fusion(f32[1024,16,128]{2,0,1:T(8,128)S(1)} %get-tuple-element.4, f32[2,2048,128]{2,1,0:T(8,128)} %collective-permute-done.1, f32[1024,2048]{1,0:T(8,128)S(1)} %copy-done), kind=kOutput, calls=%fused_computation.15 | convolution fusion | flops 6442450944 | bytes 12582912 | tf_op jit(solution)/shard_map/td,qdr->tqr/dot_general | solution.py:20
  102.8 0.0 copy-start.1
  102.8 6.9 %constant_dynamic-update-slice_fusion.5 = (f32[1024,16,128]{2,0,1:T(8,128)S(1)}, f32[1024,2,128]{2,0,1:T(8,128)S(1)}) fusion(f32[1024,16,128]{2,0,1:T(8,128)S(1)} %get-tuple-element.6, f32[2,2048,128]{2,1,0:T(8,128)S(1)} %collective-permute-done, f32[1024,2048]{1,0:T(8,128)S(1)} %copy-done), kind=kOutput, calls=%fused_computation.14 | convolution fusion | flops 6442450944 | bytes 12582912 | tf_op jit(solution)/shard_map/td,qdr->tqr/dot_general | solution.py:20
  109.7 0.0 copy-done.1
  109.7 6.7 %constant_dynamic-update-slice_fusion.4 = (f32[1024,16,128]{2,0,1:T(8,128)S(1)}, f32[1024,2,128]{2,0,1:T(8,128)S(1)}) fusion(f32[1024,16,128]{2,0,1:T(8,128)S(1)} %get-tuple-element.8, f32[2,2048,128]{2,1,0:T(8,128)S(1)} %copy-done.1, f32[1024,2048]{1,0:T(8,128)S(1)} %copy-done), kind=kOutput, calls=%fused_computation.13 | convolution fusion | flops 6442450944 | bytes 12582912 | tf_op jit(solution)/shard_map/td,qdr->tqr/dot_general | solution.py:20
  116.4 0.1 constant_dynamic-update-slice_fusion.3
  116.5 0.1 constant_dynamic-update-slice_fusion.2
  116.6 0.0 copy-start.4
  116.6 0.0 copy-start.2
  116.6 0.1 constant_dynamic-update-slice_fusion.1
  116.7 0.1 constant_dynamic-update-slice_fusion
  116.7 2.2 constant_dynamic-slice_fusion
  119.0 0.0 reduce-scatter.2.cloned.1.call-update
  119.0 0.0 copy-done.4
  119.0 0.1 convert_reduce_fusion
  119.1 78.8 %reduce-scatter.2.cloned.1.call-done = f32[256,8,128]{2,0,1:T(8,128)} async-done(((f32[1024,8,128]{2,0,1:T(8,128)}), f32[256,8,128]{2,0,1:T(8,128)}) %reduce-scatter.2.cloned.1.call-update) | async-done | bytes 1048592 | tf_op jit(solution)/shard_map/reduce_scatter | solution.py:31
  197.9 0.0 copy-done.2
  197.9 1.6 multiply_reduce_fusion
  199.5 0.0 copy-start.3
  199.5 0.1 fusion.8
  199.7 33.5 %all-reduce = (f32[16,8]{0,1:T(8,128)S(1)}, f32[16]{0:T(128)S(1)}) all-reduce(f32[16,8]{0,1:T(8,128)S(1)} %fusion.8, f32[16]{0:T(128)S(1)} %convert_reduce_fusion), channel_id=1, replica_groups=mesh['groups'=2,'blk'=4,'width'=4] {'blk','width'}, use_global_device_ids=true, to_apply=%region_2.3 | all-reduce | flops 144 | bytes 1152 | tf_op jit(solution)/shard_map/psum | solution.py:44
  233.2 0.6 broadcast_divide_fusion
  233.8 0.0 copy-done.3
  (1 shorter events, 0.0 us)
Async XLA Ops:
  7.2 190.8 %reduce-scatter.2.cloned.1.call-start = ((), (), s32[]{:S(2)}) async-start(), calls=%async_computation.1 | async-start | bytes 5242880 | tf_op jit(solution)/shard_map/reduce_scatter | solution.py:31
  7.2 26.4 %collective-permute-start = (f32[2,2048,128]{2,1,0:T(8,128)}, f32[2,2048,128]{2,1,0:T(8,128)S(1)}, u32[]{:S(2)}, u32[]{:S(2)}) collective-permute-start(f32[2,2048,128]{2,1,0:T(8,128)} %param.5), channel_id=1, source_target_pairs={{0,4},{4,8},{8,12},{12,0},{1,5},{5,9},{9,13},{13,1},{2,6},{6,10},{... | collective-permute-start | bytes 6291464 | tf_op jit(solution)/shard_map/ppermute | solution.py:15
  33.6 25.6 %collective-permute-start.1 = (f32[2,2048,128]{2,1,0:T(8,128)S(1)}, f32[2,2048,128]{2,1,0:T(8,128)}, u32[]{:S(2)}, u32[]{:S(2)}) collective-permute-start(f32[2,2048,128]{2,1,0:T(8,128)S(1)} %collective-permute-done), channel_id=1, source_target_pairs={{0,4},{4,8},{8,12},{12,0},{1,5},{5,9},{9,13},{13,1},{2,6},{6,10},{... | collective-permute-start | bytes 6291464 | tf_op jit(solution)/shard_map/ppermute | solution.py:15
  59.2 25.8 %collective-permute-start.2 = (f32[2,2048,128]{2,1,0:T(8,128)}, f32[2,2048,128]{2,1,0:T(8,128)}, u32[]{:S(2)}, u32[]{:S(2)}) collective-permute-start(f32[2,2048,128]{2,1,0:T(8,128)} %collective-permute-done.1), channel_id=1, source_target_pairs={{0,4},{4,8},{8,12},{12,0},{1,5},{5,9},{9,13},{13,1},{2,6},{6,10},{... | collective-permute-start | bytes 6291464 | tf_op jit(solution)/shard_map/ppermute | solution.py:15
  59.2 35.4 %copy-start = (f32[1024,2048]{1,0:T(8,128)S(1)}, f32[1024,2048]{1,0:T(8,128)}, u32[]{:S(2)}) copy-start(f32[1024,2048]{1,0:T(8,128)} %param.4) | copy-start | bytes 25165828
  102.8 6.9 %copy-start.1 = (f32[2,2048,128]{2,1,0:T(8,128)S(1)}, f32[2,2048,128]{2,1,0:T(8,128)}, u32[]{:S(2)}) copy-start(f32[2,2048,128]{2,1,0:T(8,128)} %param.5) | copy-start | bytes 6291460
  116.6 2.4 %copy-start.4 = (s32[256]{0:T(256)S(1)}, s32[256]{0:T(256)}, u32[]{:S(2)}) copy-start(s32[256]{0:T(256)} %param.7) | copy-start | bytes 3076
  116.6 81.4 %copy-start.2 = (f32[256,128]{1,0:T(8,128)S(1)}, f32[256,128]{1,0:T(8,128)}, u32[]{:S(2)}) copy-start(f32[256,128]{1,0:T(8,128)} %param.6) | copy-start | bytes 393220
  199.5 34.3 %copy-start.3 = (f32[256,8]{0,1:T(8,128)}, f32[256,8]{0,1:T(8,128)S(1)}, u32[]{:S(2)}) copy-start(f32[256,8]{0,1:T(8,128)S(1)} %multiply_reduce_fusion) | copy-start | bytes 24580
Sparse Core Ops, SparseCore 0:
  119.1 78.7 reduce-scatter.1
